TPU v7x, 128 devices: a whole 4x4x4 slice. The times are simulated.
128 devices in a mesh: img: 16 (over x, y_lo, core), row: 8 (over y_hi, z).
Axes of the slice: x: 4, y: 4 (y_hi: 2, y_lo: 2; y = y_hi * 2 + y_lo), z: 4, core: 2. Of those that a mesh axis runs over, the one named last changes fastest.
Arguments:
- features: bfloat16 [16, 64, 384, 256], P('img', 'row'), may hold values from -6 to 6
- cotangent: bfloat16 [16, 64, 384, 256], P('img', 'row'), may hold values from -6 to 6
- weight_one: bfloat16 [3, 3, 256, 256], replicated, may hold values from -0.125 to 0.125
- weight_two: bfloat16 [3, 3, 256, 256], replicated, may hold values from -0.125 to 0.125
Outputs:
- input_grad: bfloat16 [16, 64, 384, 256], P('img', 'row')
- weight_one_grad: float32 [589824], P(('img', 'row'))
- weight_two_grad: float32 [589824], P(('img', 'row'))
All inputs are finite; a program needn't handle non-finite values.
Results may differ from a plain program's by a relative error of at most 0.0055.
Values may be sent and summed in bfloat16 or wider, within the bound.
A program may use at most 128 MiB of HBM per device.

v0:
```python
import functools
import math

import jax
import jax.numpy as jnp
from jax import lax
from jax.experimental import pallas as pl
from jax.experimental.pallas import tpu as pltpu
from jax.sharding import PartitionSpec as P

MESH = pl.DeviceIdType.MESH
F32 = jnp.float32
BF16 = jnp.bfloat16
COEFF = 0.7978845608028654
CUBIC = 0.044715
ROWS = 8
COLS = 384
CHANS = 256
WIDE = 3 * CHANS
CELLS = ROWS * COLS
GROUP = 144
PIECE = 18


def gelu_parts(v):
    sq = v * v
    t = jnp.tanh(COEFF * v * (1.0 + CUBIC * sq))
    half = 0.5 * (1.0 + t)
    slope = half + (0.5 * COEFF) * v * (1.0 - t * t) * (1.0 + (3.0 * CUBIC) * sq)
    return v * half, slope


def shifted(v):
    index = lax.broadcasted_iota(jnp.int32, v.shape, 0)
    left = jnp.where(index == 0, 0.0, pltpu.roll(v, 1, 0))
    right = jnp.where(index == COLS - 1, 0.0, pltpu.roll(v, COLS - 1, 0))
    return left, right


def span(row):
    if isinstance(row, int):
        return pl.ds(row * COLS, COLS)
    return pl.ds(pl.multiple_of(row * COLS, COLS), COLS)


def kernel(
    scale,
    feat,
    cot,
    w_one,
    w_two,
    out,
    out_one,
    out_two,
    fv,
    gv,
    wv1,
    wv2,
    wt1,
    wt2,
    a3,
    g3,
    h3,
    at,
    gt,
    slope,
    hid,
    bh,
    hsend,
    hrecv,
    stage,
    acc,
    crecv,
    xsend,
    xrecv,
    xown,
    ysend,
    yrecv,
    yown,
    zsend,
    zrecv,
    zown,
    load_sem,
    w_sem,
    halo_send,
    halo_recv,
    out_sem,
    core_send,
    core_recv,
    ring_send,
    ring_recv,
):
    img, row = lax.axis_index("img"), lax.axis_index("row")
    core, y_lo, x = img % 2, (img // 2) % 2, img // 4
    z, y_hi = row % 4, row // 4
    y = y_hi * 2 + y_lo

    def x_peer(k):
        there = (x + k) % 4
        return there, ((there * 2 + y_lo) * 2 + core, row)

    def y_peer(k):
        there = (y + k) % 4
        return there, ((x * 2 + there % 2) * 2 + core, (there // 2) * 4 + z)

    def z_peer(k):
        there = (z + k) % 4
        return there, (img, y_hi * 4 + there)

    partner = ((x * 2 + y_lo) * 2 + (1 - core), row)
    below, above = (img, (row + 1) % 8), (img, (row + 7) % 8)

    barrier = pltpu.get_barrier_semaphore()
    peers = [partner, below, above]
    for peer in (x_peer, y_peer, z_peer):
        for k in (1, 2, 3):
            peers.append(peer(k)[1])
    for peer in peers:
        pl.semaphore_signal(barrier, inc=1, device_id=peer, device_id_type=MESH)

    loads = [
        pltpu.make_async_copy(feat.at[0, r], fv.at[span(r + 1)], load_sem.at[0, r]) for r in range(ROWS)
    ] + [pltpu.make_async_copy(cot.at[0, r], gv.at[span(r + 1)], load_sem.at[1, r]) for r in range(ROWS)]
    weights = [
        pltpu.make_async_copy(w_one, wv1, w_sem.at[0]),
        pltpu.make_async_copy(w_two, wv2, w_sem.at[1]),
    ]
    for copy in weights + loads:
        copy.start()
    pl.semaphore_wait(barrier, len(peers))

    def halo(which, down, src, dst):
        return pltpu.make_async_remote_copy(
            src_ref=src,
            dst_ref=dst,
            send_sem=halo_send.at[which, down],
            recv_sem=halo_recv.at[which, down],
            device_id=below if down else above,
            device_id_type=MESH,
        )

    halos_down = [
        halo(0, 1, feat.at[0, ROWS - 1], fv.at[span(0)]),
        halo(1, 1, cot.at[0, ROWS - 1], gv.at[span(0)]),
    ]
    halos_up = [
        halo(0, 0, feat.at[0, 0], fv.at[span(ROWS + 1)]),
        halo(1, 0, cot.at[0, 0], gv.at[span(ROWS + 1)]),
    ]
    h_down = halo(2, 1, hsend.at[1], hrecv.at[0])
    h_up = halo(2, 0, hsend.at[0], hrecv.at[1])

    @pl.when(row < 7)
    def _():
        for copy in halos_down:
            copy.start()

    @pl.when(row > 0)
    def _():
        for copy in halos_up:
            copy.start()

    for copy in weights:
        copy.wait()

    def turn(tap, _):
        a, b = tap // 3, tap % 3
        wt1[a, pl.ds(pl.multiple_of(b * CHANS, CHANS), CHANS), :] = wv1[a, b].T
        wt2[a, pl.ds(pl.multiple_of(b * CHANS, CHANS), CHANS), :] = wv2[a, b].T
        return 0

    lax.fori_loop(0, 9, turn, 0)

    def prep(r, own):
        for lane in (0, 128):
            v = fv[span(r), lane : lane + 128].astype(F32)
            acted, grade = gelu_parts(v)
            if own:
                slope[span(r - 1), lane : lane + 128] = grade
            left, right = shifted(acted)
            mid = acted.astype(BF16)
            a3[span(r), lane : lane + 128] = left.astype(BF16)
            a3[span(r), CHANS + lane : CHANS + lane + 128] = mid
            a3[span(r), 2 * CHANS + lane : 2 * CHANS + lane + 128] = right.astype(BF16)
            at[lane : lane + 128, span(r)] = mid.T
            g = gv[span(r), lane : lane + 128]
            left, right = shifted(g.astype(F32))
            g3[span(r), lane : lane + 128] = right.astype(BF16)
            g3[span(r), CHANS + lane : CHANS + lane + 128] = g
            g3[span(r), 2 * CHANS + lane : 2 * CHANS + lane + 128] = left.astype(BF16)

    for copy in loads:
        copy.wait()
    lax.fori_loop(1, ROWS + 1, lambda r, _: (prep(r, True), 0)[1], 0)

    def conv(source, weight, r, flip):
        total = None
        for a in range(3):
            near = r - a + 1 if flip else r + a - 1
            part = jnp.dot(source[span(near), :], weight(a), preferred_element_type=F32)
            total = part if total is None else total + part
        return total

    def forward_one(a):
        return wv1[a].reshape(WIDE, CHANS)

    def widen_grad(r, lane, h):
        left, right = shifted(h)
        h3[span(r), lane : lane + 128] = right.astype(BF16)
        h3[span(r), CHANS + lane : CHANS + lane + 128] = h.astype(BF16)
        h3[span(r), 2 * CHANS + lane : 2 * CHANS + lane + 128] = left.astype(BF16)

    def middle(r):
        hid[...] = conv(a3, forward_one, r, False)
        bh[...] = conv(g3, lambda a: wt2[a], r, True)
        for lane in (0, 128):
            gated, grade = gelu_parts(hid[:, lane : lane + 128])
            gt[lane : lane + 128, span(r - 1)] = gated.astype(BF16).T
            widen_grad(r, lane, bh[:, lane : lane + 128] * grade)

    lax.fori_loop(2, ROWS, lambda r, _: (middle(r), 0)[1], 0)

    @pl.when(row > 0)
    def _():
        for copy in halos_down:
            copy.wait_recv()

    @pl.when(row == 0)
    def _():
        fv[span(0), :] = jnp.zeros((COLS, CHANS), BF16)
        gv[span(0), :] = jnp.zeros((COLS, CHANS), BF16)

    @pl.when(row < 7)
    def _():
        for copy in halos_up:
            copy.wait_recv()

    @pl.when(row == 7)
    def _():
        fv[span(ROWS + 1), :] = jnp.zeros((COLS, CHANS), BF16)
        gv[span(ROWS + 1), :] = jnp.zeros((COLS, CHANS), BF16)

    lax.fori_loop(0, 2, lambda i, _: (prep(i * (ROWS + 1), False), 0)[1], 0)
    lax.fori_loop(0, 2, lambda i, _: (middle(1 + i * (ROWS - 1)), 0)[1], 0)

    hsend[0] = h3[span(1), CHANS : 2 * CHANS]
    hsend[1] = h3[span(ROWS), CHANS : 2 * CHANS]

    @pl.when(row < 7)
    def _():
        h_down.start()

    @pl.when(row > 0)
    def _():
        h_up.start()

    def core_copy(t, g):
        return pltpu.make_async_remote_copy(
            src_ref=acc.at[t, pl.ds(pl.multiple_of((2 * g + 1 - core) * GROUP, GROUP), GROUP)],
            dst_ref=crecv.at[t, g],
            send_sem=core_send.at[t, g],
            recv_sem=core_recv.at[t, g],
            device_id=partner,
            device_id_type=MESH,
        )

    def stage_copy(t, which, k):
        peer = (x_peer, y_peer, z_peer)[which]
        send, recv = ((xsend, xrecv), (ysend, yrecv), (zsend, zrecv))[which]
        there, device = peer(k)
        return pltpu.make_async_remote_copy(
            src_ref=send.at[t, there],
            dst_ref=recv.at[t, k - 1],
            send_sem=ring_send.at[t, which, k - 1],
            recv_sem=ring_recv.at[t, which, k - 1],
            device_id=device,
            device_id_type=MESH,
        )

    def core_start(t):
        for g in range(8):
            core_copy(t, g).start()

    def x_start(t):
        for g in range(8):
            core_copy(t, g).wait_recv()

        def add(g, _):
            here = pl.ds(pl.multiple_of((2 * g + core) * GROUP, GROUP), GROUP)
            total = acc[t, here, :] + crecv[t, g]
            place = pl.ds(pl.multiple_of((g % 2) * GROUP, GROUP), GROUP)
            xsend[t, g // 2, place, :] = total.astype(BF16)

            @pl.when(g // 2 == x)
            def _():
                xown[t, place, :] = total

            return 0

        lax.fori_loop(0, 8, add, 0)
        for k in (2, 1, 3):
            stage_copy(t, 0, k).start()

    def y_start(t):
        for k in (1, 2, 3):
            stage_copy(t, 0, k).wait_recv()
        for part in range(4):
            here = slice((part % 2) * GROUP + (part // 2) * 72, (part % 2) * GROUP + (part // 2) * 72 + 72)
            total = xown[t, here, :]
            for k in range(3):
                total = total + xrecv[t, k, here, :].astype(F32)
            yown[t, part] = total
            ysend[t, part] = total.astype(BF16)
        for k in (2, 1, 3):
            stage_copy(t, 1, k).start()

    def z_start(t):
        for k in (1, 2, 3):
            stage_copy(t, 1, k).wait_recv()
        total = yown[t, y]
        for k in range(3):
            total = total + yrecv[t, k].astype(F32)
        yown[t, y] = total
        for part in range(4):
            piece = yown[t, y, part * PIECE : part * PIECE + PIECE, :]
            zown[t, part] = piece
            zsend[t, part] = piece.astype(BF16)
        for k in (2, 1, 3):
            stage_copy(t, 2, k).start()

    def finish(t, result):
        for k in (1, 2, 3):
            stage_copy(t, 2, k).wait_recv()
        total = zown[t, z]
        for k in range(3):
            total = total + zrecv[t, k].astype(F32)
        result[...] = total * scale

    def grads(t, a):
        if t:
            product = jnp.dot(gt[...], g3[(2 - a) * COLS : (2 - a) * COLS + CELLS, :], preferred_element_type=F32)
        else:
            product = jnp.dot(
                at[:, a * COLS : a * COLS + CELLS], h3[COLS : COLS + CELLS, :], preferred_element_type=F32
            )
        for b in range(3):
            acc[t, (a * 3 + b) * CHANS : (a * 3 + b + 1) * CHANS, :] = product[:, b * CHANS : (b + 1) * CHANS]

    def out_copy(r):
        return pltpu.make_async_copy(stage.at[span(r - 1)], out.at[0, r - 1], out_sem.at[r - 1])

    def last(r):
        total = conv(h3, lambda a: wt1[a], r, True)
        stage[span(r - 1), :] = (
            gv[span(r), :].astype(F32) + total * slope[span(r - 1), :]
        ).astype(BF16)
        out_copy(r).start()

    def last_rows(first, end):
        lax.fori_loop(first, end, lambda r, _: (last(r), 0)[1], 0)

    for a in range(3):
        grads(1, a)
    core_start(1)
    grads(0, 0)
    x_start(1)
    grads(0, 1)
    grads(0, 2)
    core_start(0)
    last_rows(2, 4)
    x_start(0)
    last_rows(4, 6)
    y_start(1)
    last_rows(6, 8)
    z_start(1)

    @pl.when(row > 0)
    def _():
        h_down.wait_recv()

    @pl.when(row == 0)
    def _():
        hrecv[0] = jnp.zeros((COLS, CHANS), BF16)

    @pl.when(row < 7)
    def _():
        h_up.wait_recv()

    @pl.when(row == 7)
    def _():
        hrecv[1] = jnp.zeros((COLS, CHANS), BF16)

    for end in range(2):
        for lane in (0, 128):
            widen_grad(end * (ROWS + 1), lane, hrecv[end, :, lane : lane + 128].astype(F32))
    lax.fori_loop(0, 2, lambda i, _: (last(1 + i * (ROWS - 1)), 0)[1], 0)

    y_start(0)
    finish(1, out_two)
    z_start(0)
    finish(0, out_one)

    @pl.when(row < 7)
    def _():
        for copy in halos_down + [h_down]:
            copy.wait_send()

    @pl.when(row > 0)
    def _():
        for copy in halos_up + [h_up]:
            copy.wait_send()

    for r in range(ROWS):
        out_copy(r + 1).wait()
    for t in range(2):
        for g in range(8):
            core_copy(t, g).wait_send()
        for which in range(3):
            for k in (1, 2, 3):
                stage_copy(t, which, k).wait_send()


def shards(features, cotangent, weight_one, weight_two):
    height = features.shape[1] * lax.axis_size("row")
    scale = 1.0 / math.sqrt(lax.axis_size("img") * height * features.shape[2])
    hbm = pl.BlockSpec(memory_space=pl.ANY)
    vmem = pl.BlockSpec(memory_space=pltpu.VMEM)
    dma = pltpu.SemaphoreType.DMA
    wide_cells = (ROWS + 2) * COLS
    grad, one, two = pl.pallas_call(
        functools.partial(kernel, scale),
        out_shape=(
            jax.ShapeDtypeStruct(features.shape, BF16),
            jax.ShapeDtypeStruct((PIECE, CHANS), F32),
            jax.ShapeDtypeStruct((PIECE, CHANS), F32),
        ),
        in_specs=[hbm] * 4,
        out_specs=(hbm, vmem, vmem),
        scratch_shapes=[
            pltpu.VMEM((wide_cells, CHANS), BF16),
            pltpu.VMEM((wide_cells, CHANS), BF16),
            pltpu.VMEM((3, 3, CHANS, CHANS), BF16),
            pltpu.VMEM((3, 3, CHANS, CHANS), BF16),
            pltpu.VMEM((3, WIDE, CHANS), BF16),
            pltpu.VMEM((3, WIDE, CHANS), BF16),
            pltpu.VMEM((wide_cells, WIDE), BF16),
            pltpu.VMEM((wide_cells, WIDE), BF16),
            pltpu.VMEM((wide_cells, WIDE), BF16),
            pltpu.VMEM((CHANS, wide_cells), BF16),
            pltpu.VMEM((CHANS, CELLS), BF16),
            pltpu.VMEM((CELLS, CHANS), F32),
            pltpu.VMEM((COLS, CHANS), F32),
            pltpu.VMEM((COLS, CHANS), F32),
            pltpu.VMEM((2, COLS, CHANS), BF16),
            pltpu.VMEM((2, COLS, CHANS), BF16),
            pltpu.VMEM((CELLS, CHANS), BF16),
            pltpu.VMEM((2, 9 * CHANS, CHANS), F32),
            pltpu.VMEM((2, 8, GROUP, CHANS), F32),
            pltpu.VMEM((2, 4, 2 * GROUP, CHANS), BF16),
            pltpu.VMEM((2, 3, 2 * GROUP, CHANS), BF16),
            pltpu.VMEM((2, 2 * GROUP, CHANS), F32),
            pltpu.VMEM((2, 4, GROUP // 2, CHANS), BF16),
            pltpu.VMEM((2, 3, GROUP // 2, CHANS), BF16),
            pltpu.VMEM((2, 4, GROUP // 2, CHANS), F32),
            pltpu.VMEM((2, 4, PIECE, CHANS), BF16),
            pltpu.VMEM((2, 3, PIECE, CHANS), BF16),
            pltpu.VMEM((2, 4, PIECE, CHANS), F32),
            dma((2, ROWS)),
            dma((2,)),
            dma((3, 2)),
            dma((3, 2)),
            dma((ROWS,)),
            dma((2, 8)),
            dma((2, 8)),
            dma((2, 3, 3)),
            dma((2, 3, 3)),
        ],
        compiler_params=pltpu.CompilerParams(
            collective_id=0, has_side_effects=True, vmem_limit_bytes=64 * 1000 * 1000
        ),
        name="unit_backward",
    )(features, cotangent, weight_one, weight_two)
    return grad, one.reshape(-1), two.reshape(-1)


def solution(mesh):
    placed = (P("img", "row", None, None), P("img", "row", None, None), P(), P())
    return jax.shard_map(
        shards,
        mesh=mesh,
        in_specs=placed,
        out_specs=(P("img", "row", None, None), P(("img", "row")), P(("img", "row"))),
        check_vma=False,
    )
```

profile of v0, /device:TPU:0, one launch (start us, length us, event | category | flops | bytes accessed | tf_op | source)
XLA Modules:
  0.0 62.9 jit_solution(9555250988608980666)
XLA Ops:
  0.6 56.9 %unit_backward.1 = (bf16[1,8,384,256]{3,2,1,0:T(8,128)(2,1)}, f32[18,256]{1,0:T(8,128)}, f32[18,256]{1,0:T(8,128)}) custom-call(bf16[1,8,384,256]{3,2,1,0:T(8,128)(2,1)} %feat.1, bf16[1,8,384,256]{3,2,1,0:T(8,128)(2,1)} %cot.1, bf16[3,3,256,256]{3,2,1,0:T(8,128)(2,1)} %w_one.1, bf16[3,3,256,256]{3,2,1,0:T(8,128)(2,1)} %w_two.1), custom_call_target="tpu_custom_call" | custom-call | tf_op jit(solution)/shard_map/unit_backward/pallas_call | solution.py:430
  57.5 1.3 %reshape.12 = f32[4608]{0:T(1024)} reshape(f32[18,256]{1,0:T(8,128)} %get-tuple-element.7) | data formatting | bytes 36864 | tf_op jit(solution)/shard_map/reshape | solution.py:483
  58.9 1.3 %reshape.13 = f32[4608]{0:T(1024)} reshape(f32[18,256]{1,0:T(8,128)} %get-tuple-element.8) | data formatting | bytes 36864 | tf_op jit(solution)/shard_map/reshape | solution.py:483
  60.2 2.7 %copy.8 = bf16[1,8,384,256]{3,2,1,0:T(8,128)(2,1)} copy(bf16[1,8,384,256]{3,2,1,0:T(8,128)(2,1)} %get-tuple-element.12) | data formatting | bytes 3145728
where the time goes:
time: 63.1 us; the launch traced here: 62.9 us
  Pallas kernels  56.9 us (90%)
  local copies, waits for them, and re-layouts  5.34 us (8%)
  between operations  0.64 us (1%)
    pallas_call x1, Pallas kernels, shards(): pl.pallas_call(functools.partial(kernel, scale), out_shape=(jax.ShapeDtyp...  56.9 us
    reshape x2, local copies, waits for them, and re-layouts, shards(): return (grad, one.reshape(-1), two.reshape(-1))  2.69 us
    unnamed x1, local copies, waits for them, and re-layouts  2.65 us

commit v1 on v0

v1 whole, which is shorter than its diff:
```python
import functools
import math

import jax
import jax.numpy as jnp
from jax import lax
from jax.experimental import pallas as pl
from jax.experimental.pallas import tpu as pltpu
from jax.sharding import PartitionSpec as P

MESH = pl.DeviceIdType.MESH
F32 = jnp.float32
BF16 = jnp.bfloat16
COEFF = 0.7978845608028654
CUBIC = 0.044715
ROWS = 8
COLS = 384
CHANS = 256
WIDE = 3 * CHANS
CELLS = ROWS * COLS
GROUP = 144
PIECE = 18


def gelu_terms(v):
    poly = COEFF + (COEFF * CUBIC) * (v * v)
    half = 0.5 + 0.5 * jnp.tanh(v * poly)
    return v * half, half, poly


def slope_of(acted, half, poly):
    return half + acted * (1.0 - half) * (6.0 * poly - 4.0 * COEFF)


def shifted(v):
    index = lax.broadcasted_iota(jnp.int32, v.shape, 0)
    left = jnp.where(index == 0, 0.0, pltpu.roll(v, 1, 0))
    right = jnp.where(index == COLS - 1, 0.0, pltpu.roll(v, COLS - 1, 0))
    return left, right


def span(row, count=1):
    return slice(row * COLS, (row + count) * COLS)


def kernel(
    scale,
    feat,
    cot,
    w_one,
    w_two,
    out,
    out_one,
    out_two,
    fv,
    gv,
    wv1,
    wv2,
    wt1,
    wt2,
    a3,
    g3,
    h3,
    at,
    gt,
    slope,
    hid,
    bh,
    hsend,
    hrecv,
    stage,
    acc,
    crecv,
    send1,
    recv1,
    own1,
    send2,
    recv2,
    own2,
    send3,
    recv3,
    own3,
    load_sem,
    w_sem,
    halo_send,
    halo_recv,
    out_sem,
    core_send,
    core_recv,
    wide_send,
    wide_recv,
    last_send,
    last_recv,
):
    img, row = lax.axis_index("img"), lax.axis_index("row")
    core, y_lo, x = img % 2, (img // 2) % 2, img // 4
    z, y_hi = row % 4, row // 4
    y = y_hi * 2 + y_lo

    def x_peer(k):
        there = (x + k) % 4
        return there, ((there * 2 + y_lo) * 2 + core, row)

    def y_peer(k):
        there = (y + k) % 4
        return there, ((x * 2 + there % 2) * 2 + core, (there // 2) * 4 + z)

    def z_peer(k):
        there = (z + k) % 4
        return there, (img, y_hi * 4 + there)

    partner = ((x * 2 + y_lo) * 2 + (1 - core), row)
    below, above = (img, (row + 1) % 8), (img, (row + 7) % 8)

    loads = [
        (
            pltpu.make_async_copy(feat.at[0, r], fv.at[span(r + 1)], load_sem.at[0, r]),
            pltpu.make_async_copy(cot.at[0, r], gv.at[span(r + 1)], load_sem.at[1, r]),
        )
        for r in range(ROWS)
    ]
    weights = [
        pltpu.make_async_copy(w_one, wv1, w_sem.at[0]),
        pltpu.make_async_copy(w_two, wv2, w_sem.at[1]),
    ]
    for pair in loads[:4]:
        for copy in pair:
            copy.start()
    for copy in weights:
        copy.start()
    for pair in loads[4:]:
        for copy in pair:
            copy.start()

    barrier = pltpu.get_barrier_semaphore()
    peers = [partner, below, above]
    for peer in (x_peer, y_peer, z_peer):
        for k in (1, 2, 3):
            peers.append(peer(k)[1])
    for peer in peers:
        pl.semaphore_signal(barrier, inc=1, device_id=peer, device_id_type=MESH)
    pl.semaphore_wait(barrier, len(peers))

    def halo(which, down, src, dst):
        return pltpu.make_async_remote_copy(
            src_ref=src,
            dst_ref=dst,
            send_sem=halo_send.at[which, down],
            recv_sem=halo_recv.at[which, down],
            device_id=below if down else above,
            device_id_type=MESH,
        )

    halos_down = [
        halo(0, 1, feat.at[0, ROWS - 1], fv.at[span(0)]),
        halo(1, 1, cot.at[0, ROWS - 1], gv.at[span(0)]),
    ]
    halos_up = [
        halo(0, 0, feat.at[0, 0], fv.at[span(ROWS + 1)]),
        halo(1, 0, cot.at[0, 0], gv.at[span(ROWS + 1)]),
    ]
    h_down = halo(2, 1, hsend.at[1], hrecv.at[0])
    h_up = halo(2, 0, hsend.at[0], hrecv.at[1])

    @pl.when(row < 7)
    def _():
        for copy in halos_down:
            copy.start()

    @pl.when(row > 0)
    def _():
        for copy in halos_up:
            copy.start()

    def turn(source, target):
        for a in range(3):
            for b in range(3):
                target[a, b * CHANS : (b + 1) * CHANS, :] = source[a, b].T

    def prep(r):
        for lane in (0, 128):
            acted, _, _ = gelu_terms(fv[span(r), lane : lane + 128].astype(F32))
            left, right = shifted(acted)
            mid = acted.astype(BF16)
            a3[span(r), lane : lane + 128] = left.astype(BF16)
            a3[span(r), CHANS + lane : CHANS + lane + 128] = mid
            a3[span(r), 2 * CHANS + lane : 2 * CHANS + lane + 128] = right.astype(BF16)
            at[lane : lane + 128, span(r)] = mid.T
            g = gv[span(r), lane : lane + 128]
            left, right = shifted(g.astype(F32))
            g3[span(r), lane : lane + 128] = right.astype(BF16)
            g3[span(r), CHANS + lane : CHANS + lane + 128] = g
            g3[span(r), 2 * CHANS + lane : 2 * CHANS + lane + 128] = left.astype(BF16)

    def grade(r):
        for lane in (0, 128):
            slope[span(r - 1), lane : lane + 128] = slope_of(
                *gelu_terms(fv[span(r), lane : lane + 128].astype(F32))
            )

    def conv(source, weight, r, count, flip):
        total = None
        for a in range(3):
            near = r - a + 1 if flip else r + a - 1
            part = jnp.dot(source[span(near, count), :], weight(a), preferred_element_type=F32)
            total = part if total is None else total + part
        return total

    def forward_one(a):
        return wv1[a].reshape(WIDE, CHANS)

    def convs(r, count, slot):
        hid[slot, : count * COLS, :] = conv(a3, forward_one, r, count, False)
        bh[slot, : count * COLS, :] = conv(g3, lambda a: wt2[a], r, count, True)

    def widen_grad(r, lane, h):
        left, right = shifted(h)
        h3[span(r), lane : lane + 128] = right.astype(BF16)
        h3[span(r), CHANS + lane : CHANS + lane + 128] = h.astype(BF16)
        h3[span(r), 2 * CHANS + lane : 2 * CHANS + lane + 128] = left.astype(BF16)

    def elem(r, slot, part):
        for lane in (0, 128):
            terms = gelu_terms(hid[slot, span(part), lane : lane + 128])
            gt[lane : lane + 128, span(r - 1)] = terms[0].astype(BF16).T
            widen_grad(r, lane, bh[slot, span(part), lane : lane + 128] * slope_of(*terms))

    def grads(t, a, r, count, fresh):
        if t:
            left, right = gt[:, span(r - 1, count)], g3[span(r - a + 1, count), :]
        else:
            left, right = at[:, span(r + a - 1, count)], h3[span(r, count), :]
        product = jnp.dot(left, right, preferred_element_type=F32)
        for b in range(3):
            here = slice((a * 3 + b) * CHANS, (a * 3 + b + 1) * CHANS)
            piece = product[:, b * CHANS : (b + 1) * CHANS]
            acc[t, here, :] = piece if fresh else acc[t, here, :] + piece

    def core_copy(t, g):
        return pltpu.make_async_remote_copy(
            src_ref=acc.at[t, pl.ds(pl.multiple_of((2 * g + 1 - core) * GROUP, GROUP), GROUP)],
            dst_ref=crecv.at[t, g],
            send_sem=core_send.at[t, g],
            recv_sem=core_recv.at[t, g],
            device_id=partner,
            device_id_type=MESH,
        )

    def wide_copy(t, color, step, k):
        send, recv = ((send1, recv1), (send2, recv2))[step]
        there, device = (x_peer if color == step else y_peer)(k)
        return pltpu.make_async_remote_copy(
            src_ref=send.at[t, color, there],
            dst_ref=recv.at[t, color, k - 1],
            send_sem=wide_send.at[t, color, step, k - 1],
            recv_sem=wide_recv.at[t, color, step, k - 1],
            device_id=device,
            device_id_type=MESH,
        )

    def last_copy(t, k):
        there, device = z_peer(k)
        return pltpu.make_async_remote_copy(
            src_ref=send3.at[t, there],
            dst_ref=recv3.at[t, k - 1],
            send_sem=last_send.at[t, k - 1],
            recv_sem=last_recv.at[t, k - 1],
            device_id=device,
            device_id_type=MESH,
        )

    HALF = GROUP // 2
    LEFT, RIGHT = slice(0, 128), slice(128, 256)

    def core_start(t, a):
        for g in ((0, 1), (2, 3, 4), (5, 6, 7))[a]:
            core_copy(t, g).start()

    def core_add(t, a):
        for g in ((0, 1), (2, 3, 4), (5, 6, 7))[a]:
            core_copy(t, g).wait_recv()
            here = pl.ds(pl.multiple_of((2 * g + core) * GROUP, GROUP), GROUP)
            total = acc[t, here, :] + crecv[t, g]
            crecv[t, g] = total
            place, low = g // 2, g % 2
            send1[t, 0, place, low * GROUP : (low + 1) * GROUP, :] = total[:, LEFT].astype(BF16)
            for high in range(2):
                send1[t, 1, high * 2 + low, place * HALF : (place + 1) * HALF, :] = total[
                    high * HALF : (high + 1) * HALF, RIGHT
                ].astype(BF16)

    def start1(t):
        for k in (2, 1, 3):
            for color in range(2):
                wide_copy(t, color, 0, k).start()

    def start2(t):
        for color in range(2):
            for k in (1, 2, 3):
                wide_copy(t, color, 0, k).wait_recv()
        for low in range(2):
            for high in range(2):
                rows = slice(low * GROUP + high * HALF, low * GROUP + (high + 1) * HALF)
                total = crecv[t, 2 * x + low, high * HALF : (high + 1) * HALF, LEFT]
                for k in range(3):
                    total = total + recv1[t, 0, k, rows, :].astype(F32)
                own1[t, 0, high * 2 + low] = total
                send2[t, 0, high * 2 + low] = total.astype(BF16)
        for place in range(4):
            rows = slice(place * HALF, (place + 1) * HALF)
            total = crecv[t, 2 * place + y_lo, pl.ds(pl.multiple_of(y_hi * HALF, HALF), HALF), RIGHT]
            for k in range(3):
                total = total + recv1[t, 1, k, rows, :].astype(F32)
            own1[t, 1, place] = total
            send2[t, 1, place] = total.astype(BF16)
        for k in (2, 1, 3):
            for color in range(2):
                wide_copy(t, color, 1, k).start()

    def start3(t):
        for color, mine in ((0, y), (1, x)):
            for k in (1, 2, 3):
                wide_copy(t, color, 1, k).wait_recv()
            total = own1[t, color, mine]
            for k in range(3):
                total = total + recv2[t, color, k].astype(F32)
            own2[t, color] = total
            lanes = (LEFT, RIGHT)[color]
            for part in range(4):
                piece = own2[t, color, part * PIECE : part * PIECE + PIECE, :]
                own3[t, part, :, lanes] = piece
                send3[t, part, :, lanes] = piece.astype(BF16)
        for k in (2, 1, 3):
            last_copy(t, k).start()

    def finish(t, result):
        for k in (1, 2, 3):
            last_copy(t, k).wait_recv()
        total = own3[t, z]
        for k in range(3):
            total = total + recv3[t, k].astype(F32)
        total = total * scale
        result[pl.ds(0, PIECE, stride=2), :] = total[:, LEFT]
        result[pl.ds(1, PIECE, stride=2), :] = total[:, RIGHT]

    def out_copy(r):
        return pltpu.make_async_copy(stage.at[span(r - 1)], out.at[0, r - 1], out_sem.at[r - 1])

    def last(r, count):
        total = conv(h3, lambda a: wt1[a], r, count, True)
        here = span(r - 1, count)
        stage[here, :] = (gv[span(r, count), :].astype(F32) + total * slope[here, :]).astype(BF16)
        for k in range(count):
            out_copy(r + k).start()

    for pair in loads[:4]:
        for copy in pair:
            copy.wait()
    for copy in weights:
        copy.wait()
    turn(wv2, wt2)
    for r in (1, 2, 3, 4):
        prep(r)
    for pair in loads[4:]:
        for copy in pair:
            copy.wait()
    convs(2, 2, 0)
    prep(5)
    prep(6)
    convs(4, 2, 1)
    elem(2, 0, 0)
    elem(3, 0, 1)
    prep(7)
    prep(8)
    convs(6, 2, 0)
    elem(4, 1, 0)
    elem(5, 1, 1)

    @pl.when(row > 0)
    def _():
        for copy in halos_down:
            copy.wait_recv()

    @pl.when(row == 0)
    def _():
        fv[span(0), :] = jnp.zeros((COLS, CHANS), BF16)
        gv[span(0), :] = jnp.zeros((COLS, CHANS), BF16)

    @pl.when(row < 7)
    def _():
        for copy in halos_up:
            copy.wait_recv()

    @pl.when(row == 7)
    def _():
        fv[span(ROWS + 1), :] = jnp.zeros((COLS, CHANS), BF16)
        gv[span(ROWS + 1), :] = jnp.zeros((COLS, CHANS), BF16)

    for a in range(3):
        grads(1, a, 2, 4, True)
    prep(0)
    prep(ROWS + 1)
    turn(wv1, wt1)
    convs(1, 1, 1)
    elem(6, 0, 0)
    convs(ROWS, 1, 2)
    elem(7, 0, 1)
    for a in range(3):
        grads(1, a, 6, 2, False)
    elem(1, 1, 0)
    elem(ROWS, 2, 0)
    hsend[0] = h3[span(1), CHANS : 2 * CHANS]
    hsend[1] = h3[span(ROWS), CHANS : 2 * CHANS]

    @pl.when(row < 7)
    def _():
        h_down.start()

    @pl.when(row > 0)
    def _():
        h_up.start()

    for a in range(3):
        grads(1, a, 1, 1, False)
        grads(1, a, ROWS, 1, False)
        core_start(1, a)
        grade(1 + a)
    grads(0, 0, 1, ROWS, True)
    core_start(0, 0)
    grade(4)
    grade(5)
    for a in range(3):
        core_add(1, a)
    start1(1)
    grads(0, 1, 1, ROWS, True)
    core_start(0, 1)
    grade(6)
    grade(7)
    grads(0, 2, 1, ROWS, True)
    core_start(0, 2)
    core_add(0, 0)
    core_add(0, 1)
    grade(8)
    last(2, 2)
    core_add(0, 2)
    start1(0)
    start2(1)
    last(4, 2)
    start3(1)
    last(6, 2)

    @pl.when(row > 0)
    def _():
        h_down.wait_recv()

    @pl.when(row == 0)
    def _():
        hrecv[0] = jnp.zeros((COLS, CHANS), BF16)

    @pl.when(row < 7)
    def _():
        h_up.wait_recv()

    @pl.when(row == 7)
    def _():
        hrecv[1] = jnp.zeros((COLS, CHANS), BF16)

    start2(0)
    for end in range(2):
        for lane in (0, 128):
            widen_grad(end * (ROWS + 1), lane, hrecv[end, :, lane : lane + 128].astype(F32))
    last(1, 1)
    finish(1, out_two)
    start3(0)
    last(ROWS, 1)
    finish(0, out_one)

    @pl.when(row < 7)
    def _():
        for copy in halos_down + [h_down]:
            copy.wait_send()

    @pl.when(row > 0)
    def _():
        for copy in halos_up + [h_up]:
            copy.wait_send()

    for r in range(ROWS):
        out_copy(r + 1).wait()
    for t in range(2):
        for g in range(8):
            core_copy(t, g).wait_send()
        for k in (1, 2, 3):
            for color in range(2):
                for step in range(2):
                    wide_copy(t, color, step, k).wait_send()
            last_copy(t, k).wait_send()


def shards(features, cotangent, weight_one, weight_two):
    height = features.shape[1] * lax.axis_size("row")
    scale = 1.0 / math.sqrt(lax.axis_size("img") * height * features.shape[2])
    hbm = pl.BlockSpec(memory_space=pl.ANY)
    vmem = pl.BlockSpec(memory_space=pltpu.VMEM)
    dma = pltpu.SemaphoreType.DMA
    wide_cells = (ROWS + 2) * COLS
    grad, one, two = pl.pallas_call(
        functools.partial(kernel, scale),
        out_shape=(
            jax.ShapeDtypeStruct(features.shape, BF16),
            jax.ShapeDtypeStruct((2 * PIECE, 128), F32),
            jax.ShapeDtypeStruct((2 * PIECE, 128), F32),
        ),
        in_specs=[hbm] * 4,
        out_specs=(hbm, vmem, vmem),
        scratch_shapes=[
            pltpu.VMEM((wide_cells, CHANS), BF16),
            pltpu.VMEM((wide_cells, CHANS), BF16),
            pltpu.VMEM((3, 3, CHANS, CHANS), BF16),
            pltpu.VMEM((3, 3, CHANS, CHANS), BF16),
            pltpu.VMEM((3, WIDE, CHANS), BF16),
            pltpu.VMEM((3, WIDE, CHANS), BF16),
            pltpu.VMEM((wide_cells, WIDE), BF16),
            pltpu.VMEM((wide_cells, WIDE), BF16),
            pltpu.VMEM((wide_cells, WIDE), BF16),
            pltpu.VMEM((CHANS, wide_cells), BF16),
            pltpu.VMEM((CHANS, CELLS), BF16),
            pltpu.VMEM((CELLS, CHANS), F32),
            pltpu.VMEM((3, 2 * COLS, CHANS), F32),
            pltpu.VMEM((3, 2 * COLS, CHANS), F32),
            pltpu.VMEM((2, COLS, CHANS), BF16),
            pltpu.VMEM((2, COLS, CHANS), BF16),
            pltpu.VMEM((CELLS, CHANS), BF16),
            pltpu.VMEM((2, 9 * CHANS, CHANS), F32),
            pltpu.VMEM((2, 8, GROUP, CHANS), F32),
            pltpu.VMEM((2, 2, 4, 2 * GROUP, 128), BF16),
            pltpu.VMEM((2, 2, 3, 2 * GROUP, 128), BF16),
            pltpu.VMEM((2, 2, 4, GROUP // 2, 128), F32),
            pltpu.VMEM((2, 2, 4, GROUP // 2, 128), BF16),
            pltpu.VMEM((2, 2, 3, GROUP // 2, 128), BF16),
            pltpu.VMEM((2, 2, GROUP // 2, 128), F32),
            pltpu.VMEM((2, 4, PIECE, CHANS), BF16),
            pltpu.VMEM((2, 3, PIECE, CHANS), BF16),
            pltpu.VMEM((2, 4, PIECE, CHANS), F32),
            dma((2, ROWS)),
            dma((2,)),
            dma((3, 2)),
            dma((3, 2)),
            dma((ROWS,)),
            dma((2, 8)),
            dma((2, 8)),
            dma((2, 2, 2, 3)),
            dma((2, 2, 2, 3)),
            dma((2, 3)),
            dma((2, 3)),
        ],
        compiler_params=pltpu.CompilerParams(
            collective_id=0, has_side_effects=True, vmem_limit_bytes=64 * 1000 * 1000
        ),
        name="unit_backward",
    )(features, cotangent, weight_one, weight_two)
    return grad, one.reshape(-1), two.reshape(-1)


def solution(mesh):
    placed = (P("img", "row", None, None), P("img", "row", None, None), P(), P())
    return jax.shard_map(
        shards,
        mesh=mesh,
        in_specs=placed,
        out_specs=(P("img", "row", None, None), P(("img", "row")), P(("img", "row"))),
        check_vma=False,
    )
```

time: 63.1 us -> 57.8 us (0.916)
  Pallas kernels: 56.9 us -> 53.1 us
  local copies, waits for them, and re-layouts: 5.34 us -> 3.89 us
    pallas_call x1, Pallas kernels: 56.9 us -> 53.1 us  [shards(): pl.pallas_call(functools.partial(kernel, scale), out_shape=(jax.ShapeDtyp...]
    reshape x2 -> x0, local copies, waits for them, and re-layouts: 2.69 us -> none  [shards(): return (grad, one.reshape(-1), two.reshape(-1))]
    unnamed x1 -> x7, local copies, waits for them, and re-layouts: 2.65 us -> 3.89 us
where the time goes in v1:
time: 57.8 us; the launch traced here: 57.7 us
  Pallas kernels  53.1 us (92%)
  local copies, waits for them, and re-layouts  3.89 us (7%)
  between operations  0.66 us (1%)
    pallas_call x1, Pallas kernels, shards(): pl.pallas_call(functools.partial(kernel, scale), out_shape=(jax.ShapeDtyp...  53.1 us
    unnamed x7, local copies, waits for them, and re-layouts  3.89 us

profile of v1, /device:TPU:0, one launch (start us, length us, event | category | flops | bytes accessed | tf_op | source)
XLA Modules:
  0.0 57.7 jit_solution(2472262529735283695)
XLA Ops:
  0.6 53.1 %unit_backward.1 = (bf16[1,8,384,256]{3,2,1,0:T(8,128)(2,1)}, f32[36,128]{1,0:T(8,128)}, f32[36,128]{1,0:T(8,128)}) custom-call(bf16[1,8,384,256]{3,2,1,0:T(8,128)(2,1)} %feat.1, bf16[1,8,384,256]{3,2,1,0:T(8,128)(2,1)} %cot.1, bf16[3,3,256,256]{3,2,1,0:T(8,128)(2,1)} %w_one.1, bf16[3,3,256,256]{3,2,1,0:T(8,128)(2,1)} %w_two.1), custom_call_target="tpu_custom_call" | custom-call | tf_op jit(solution)/shard_map/unit_backward/pallas_call | solution.py:507
  53.8 0.0 copy-start.1
  53.8 0.0 copy-start
  53.8 2.7 %copy.10 = bf16[1,8,384,256]{3,2,1,0:T(8,128)(2,1)} copy(bf16[1,8,384,256]{3,2,1,0:T(8,128)(2,1)} %get-tuple-element.12) | data formatting | bytes 3145728
  56.5 0.0 copy-done.1
  56.5 0.6 %copy.11 = f32[4608]{0:T(1024)} copy(f32[4608]{0:T(1024)S(1)} %bitcast.3) | data formatting | bytes 36864
  57.1 0.0 copy-done
  57.1 0.6 %copy.12 = f32[4608]{0:T(1024)} copy(f32[4608]{0:T(1024)S(1)} %bitcast.2) | data formatting | bytes 36864
Async XLA Ops:
  53.8 2.7 %copy-start.1 = (f32[36,128]{1,0:T(8,128)S(1)}, f32[36,128]{1,0:T(8,128)}, u32[]{:S(2)}) copy-start(f32[36,128]{1,0:T(8,128)} %get-tuple-element.7) | copy-start | bytes 55300
  53.8 3.3 %copy-start = (f32[36,128]{1,0:T(8,128)S(1)}, f32[36,128]{1,0:T(8,128)}, u32[]{:S(2)}) copy-start(f32[36,128]{1,0:T(8,128)} %get-tuple-element.8) | copy-start | bytes 55300

commit v2 on v1

--- a/solution.py
+++ b/solution.py
@@ -32,15 +32,27 @@
     return half + acted * (1.0 - half) * (6.0 * poly - 4.0 * COEFF)
 
 
-def shifted(v):
-    index = lax.broadcasted_iota(jnp.int32, v.shape, 0)
-    left = jnp.where(index == 0, 0.0, pltpu.roll(v, 1, 0))
-    right = jnp.where(index == COLS - 1, 0.0, pltpu.roll(v, COLS - 1, 0))
-    return left, right
-
-
 def span(row, count=1):
     return slice(row * COLS, (row + count) * COLS)
+
+
+def rows_of(refs, rows, columns):
+    return jnp.concatenate([refs[r][:, columns] for r in rows], axis=0)
+
+
+def lanes_of(refs, rows):
+    return jnp.concatenate([refs[r][...] for r in rows], axis=1)
+
+
+def weave(*streams):
+    longest = max(len(stream) for stream in streams)
+    done = [0] * len(streams)
+    for step in range(longest):
+        for k, stream in enumerate(streams):
+            end = (step + 1) * len(stream) // longest
+            for task in stream[done[k] : end]:
+                task()
+            done[k] = end
 
 
 def kernel(
@@ -114,8 +126,8 @@
 
     loads = [
         (
-            pltpu.make_async_copy(feat.at[0, r], fv.at[span(r + 1)], load_sem.at[0, r]),
-            pltpu.make_async_copy(cot.at[0, r], gv.at[span(r + 1)], load_sem.at[1, r]),
+            pltpu.make_async_copy(feat.at[0, r], fv[r + 1], load_sem.at[0, r]),
+            pltpu.make_async_copy(cot.at[0, r], gv[r + 1], load_sem.at[1, r]),
         )
         for r in range(ROWS)
     ]
@@ -152,12 +164,12 @@
         )
 
     halos_down = [
-        halo(0, 1, feat.at[0, ROWS - 1], fv.at[span(0)]),
-        halo(1, 1, cot.at[0, ROWS - 1], gv.at[span(0)]),
+        halo(0, 1, feat.at[0, ROWS - 1], fv[0]),
+        halo(1, 1, cot.at[0, ROWS - 1], gv[0]),
     ]
     halos_up = [
-        halo(0, 0, feat.at[0, 0], fv.at[span(ROWS + 1)]),
-        halo(1, 0, cot.at[0, 0], gv.at[span(ROWS + 1)]),
+        halo(0, 0, feat.at[0, 0], fv[ROWS + 1]),
+        halo(1, 0, cot.at[0, 0], gv[ROWS + 1]),
     ]
     h_down = halo(2, 1, hsend.at[1], hrecv.at[0])
     h_up = halo(2, 0, hsend.at[0], hrecv.at[1])
@@ -173,68 +185,160 @@
             copy.start()
 
     def turn(source, target):
-        for a in range(3):
-            for b in range(3):
-                target[a, b * CHANS : (b + 1) * CHANS, :] = source[a, b].T
-
-    def prep(r):
-        for lane in (0, 128):
-            acted, _, _ = gelu_terms(fv[span(r), lane : lane + 128].astype(F32))
-            left, right = shifted(acted)
-            mid = acted.astype(BF16)
-            a3[span(r), lane : lane + 128] = left.astype(BF16)
-            a3[span(r), CHANS + lane : CHANS + lane + 128] = mid
-            a3[span(r), 2 * CHANS + lane : 2 * CHANS + lane + 128] = right.astype(BF16)
-            at[lane : lane + 128, span(r)] = mid.T
-            g = gv[span(r), lane : lane + 128]
-            left, right = shifted(g.astype(F32))
-            g3[span(r), lane : lane + 128] = right.astype(BF16)
-            g3[span(r), CHANS + lane : CHANS + lane + 128] = g
-            g3[span(r), 2 * CHANS + lane : 2 * CHANS + lane + 128] = left.astype(BF16)
-
-    def grade(r):
-        for lane in (0, 128):
-            slope[span(r - 1), lane : lane + 128] = slope_of(
-                *gelu_terms(fv[span(r), lane : lane + 128].astype(F32))
-            )
-
-    def conv(source, weight, r, count, flip):
-        total = None
-        for a in range(3):
-            near = r - a + 1 if flip else r + a - 1
-            part = jnp.dot(source[span(near, count), :], weight(a), preferred_element_type=F32)
-            total = part if total is None else total + part
-        return total
-
-    def forward_one(a):
-        return wv1[a].reshape(WIDE, CHANS)
-
-    def convs(r, count, slot):
-        hid[slot, : count * COLS, :] = conv(a3, forward_one, r, count, False)
-        bh[slot, : count * COLS, :] = conv(g3, lambda a: wt2[a], r, count, True)
-
-    def widen_grad(r, lane, h):
-        left, right = shifted(h)
-        h3[span(r), lane : lane + 128] = right.astype(BF16)
-        h3[span(r), CHANS + lane : CHANS + lane + 128] = h.astype(BF16)
-        h3[span(r), 2 * CHANS + lane : 2 * CHANS + lane + 128] = left.astype(BF16)
-
-    def elem(r, slot, part):
-        for lane in (0, 128):
-            terms = gelu_terms(hid[slot, span(part), lane : lane + 128])
-            gt[lane : lane + 128, span(r - 1)] = terms[0].astype(BF16).T
-            widen_grad(r, lane, bh[slot, span(part), lane : lane + 128] * slope_of(*terms))
-
-    def grads(t, a, r, count, fresh):
-        if t:
-            left, right = gt[:, span(r - 1, count)], g3[span(r - a + 1, count), :]
-        else:
-            left, right = at[:, span(r + a - 1, count)], h3[span(r, count), :]
-        product = jnp.dot(left, right, preferred_element_type=F32)
-        for b in range(3):
-            here = slice((a * 3 + b) * CHANS, (a * 3 + b + 1) * CHANS)
-            piece = product[:, b * CHANS : (b + 1) * CHANS]
-            acc[t, here, :] = piece if fresh else acc[t, here, :] + piece
+        def block(a, b):
+            target[a, b * CHANS : (b + 1) * CHANS, :] = source[a, b].T
+
+        return [functools.partial(block, a, b) for a in range(3) for b in range(3)]
+
+    def window(ref, lane, c):
+        blank = jnp.zeros((8, 128), F32)
+        low, high = 128 * c - 8, 128 * c + 136
+        inside = ref[max(low, 0) : min(high, COLS), lane : lane + 128].astype(F32)
+        if c == 0:
+            inside = jnp.concatenate([blank, inside], axis=0)
+        if c == 2:
+            inside = jnp.concatenate([inside, blank], axis=0)
+        return pltpu.roll(inside, 1, 0)[8:136], pltpu.roll(inside, 143, 0)[8:136]
+
+    def block(lane, c):
+        return slice(128 * c, 128 * c + 128), slice(lane, lane + 128)
+
+    def wide_block(lane, c, tap):
+        return slice(128 * c, 128 * c + 128), slice(tap * CHANS + lane, tap * CHANS + lane + 128)
+
+    def acted_one(r, lane, c):
+        acted, _, _ = gelu_terms(fv[r][block(lane, c)].astype(F32))
+        mid = acted.astype(BF16)
+        hid[r][block(lane, c)] = acted
+        a3[r][wide_block(lane, c, 1)] = mid
+        at[r][lane : lane + 128, 128 * c : 128 * c + 128] = mid.T
+
+    def acted_two(r, lane, c):
+        left, right = window(hid[r], lane, c)
+        a3[r][wide_block(lane, c, 0)] = left.astype(BF16)
+        a3[r][wide_block(lane, c, 2)] = right.astype(BF16)
+
+    def cot_one(r, lane, c):
+        left, right = window(gv[r], lane, c)
+        g3[r][wide_block(lane, c, 0)] = right.astype(BF16)
+        g3[r][wide_block(lane, c, 1)] = gv[r][block(lane, c)]
+        g3[r][wide_block(lane, c, 2)] = left.astype(BF16)
+
+    def grade_one(r, lane, c):
+        slope[r][block(lane, c)] = slope_of(*gelu_terms(fv[r][block(lane, c)].astype(F32)))
+
+    def elem_one(r, lane, c):
+        terms = gelu_terms(hid[r][block(lane, c)])
+        gt[r][lane : lane + 128, 128 * c : 128 * c + 128] = terms[0].astype(BF16).T
+        grad = bh[r][block(lane, c)] * slope_of(*terms)
+        bh[r][block(lane, c)] = grad
+        h3[r][wide_block(lane, c, 1)] = grad.astype(BF16)
+
+    def elem_two(r, lane, c):
+        left, right = window(bh[r], lane, c)
+        h3[r][wide_block(lane, c, 0)] = right.astype(BF16)
+        h3[r][wide_block(lane, c, 2)] = left.astype(BF16)
+
+    def halo_one(r, lane, c):
+        left, right = window(hrecv.at[r // ROWS], lane, c)
+        h3[r][wide_block(lane, c, 0)] = right.astype(BF16)
+        h3[r][wide_block(lane, c, 1)] = hrecv[r // ROWS, 128 * c : 128 * c + 128, lane : lane + 128]
+        h3[r][wide_block(lane, c, 2)] = left.astype(BF16)
+
+    def single(task, *rows):
+        return [functools.partial(task, r, lane, c) for r in rows for lane in (0, 128) for c in range(3)]
+
+    def double(one, two, *rows):
+        order = ((one, 0), (one, 1), (two, 0), (one, 2), (two, 1), (two, 2))
+        return [functools.partial(f, r, lane, c) for r in rows for lane in (0, 128) for f, c in order]
+
+    def acted(*rows):
+        return double(acted_one, acted_two, *rows)
+
+    def elem(*rows):
+        return double(elem_one, elem_two, *rows)
+
+    def cots(*rows):
+        return single(cot_one, *rows)
+
+    def grade(*rows):
+        return single(grade_one, *rows)
+
+    def both(*streams):
+        def step(tasks):
+            for task in tasks:
+                task()
+
+        return [functools.partial(step, tasks) for tasks in zip(*streams, strict=True)]
+
+    def conv(source, weight, rows, flip, keep):
+        box = [None]
+
+        def step(a, b):
+            near = [r - a + 1 if flip else r + a - 1 for r in rows]
+            columns = slice(b * CHANS, (b + 1) * CHANS)
+            part = jnp.dot(rows_of(source, near, columns), weight(a, b), preferred_element_type=F32)
+            box[0] = part if box[0] is None else box[0] + part
+            if (a, b) == (2, 2):
+                keep(box[0])
+
+        return [functools.partial(step, a, b) for a in range(3) for b in range(3)]
+
+    def keep_in(refs, rows):
+        def keep(total):
+            for k, r in enumerate(rows):
+                refs[r][...] = total[span(k), :]
+
+        return keep
+
+    def forward(*rows):
+        return conv(a3, lambda a, b: wv1[a, b], rows, False, keep_in(hid, rows))
+
+    def backward(*rows):
+        return conv(
+            g3, lambda a, b: wt2[a, b * CHANS : (b + 1) * CHANS, :], rows, True, keep_in(bh, rows)
+        )
+
+    def grads(t, fresh, terms, taps=(0, 1, 2)):
+        tall = len(taps) * CHANS
+
+        def build(b, low, high):
+            box = [None]
+
+            def step(pair, part, final):
+                lhs = jnp.concatenate([lanes_of(*pair[k]) for k in range(len(taps))], axis=0)[low:high]
+                rhs = rows_of(pair[-1][0], pair[-1][1], slice(b * CHANS, (b + 1) * CHANS))
+                deep = slice(part * CHANS, (part + 1) * CHANS)
+                product = jnp.dot(lhs[:, deep], rhs[deep, :], preferred_element_type=F32)
+                box[0] = product if box[0] is None else box[0] + product
+                if final:
+                    for k, a in enumerate(taps):
+                        start, end = max(low, k * CHANS), min(high, (k + 1) * CHANS)
+                        if start < end:
+                            base = (a * 3 + b) * CHANS - k * CHANS
+                            here = slice(base + start, base + end)
+                            piece = box[0][start - low : end - low, :]
+                            acc[t, here, :] = piece if fresh else acc[t, here, :] + piece
+
+            return [
+                functools.partial(step, pair, part, pair is terms[-1] and part == 2)
+                for pair in terms
+                for part in range(3)
+            ]
+
+        half = tall // 2
+        return both(build(0, 0, tall), build(1, 0, tall)) + both(build(2, 0, half), build(2, half, tall))
+
+    def one_grads(fresh, *pairs):
+        terms = [[(at, (p + a - 1, q + a - 1)) for a in range(3)] + [(h3, (p, q))] for p, q in pairs]
+        return grads(0, fresh, terms)
+
+    def two_grads(*pairs):
+        terms = [[(gt, (p + a - 1, q + a - 1)) for a in range(3)] + [(g3, (p, q))] for p, q in pairs]
+        return grads(1, True, terms)
+
+    def two_edge(a, left, right):
+        return grads(1, False, [[(gt, left), (g3, right)]], (a,))
 
     def core_copy(t, g):
         return pltpu.make_async_remote_copy(
@@ -272,22 +376,21 @@
     HALF = GROUP // 2
     LEFT, RIGHT = slice(0, 128), slice(128, 256)
 
-    def core_start(t, a):
-        for g in ((0, 1), (2, 3, 4), (5, 6, 7))[a]:
+    def core_start(t):
+        for g in range(8):
             core_copy(t, g).start()
 
-    def core_add(t, a):
-        for g in ((0, 1), (2, 3, 4), (5, 6, 7))[a]:
-            core_copy(t, g).wait_recv()
-            here = pl.ds(pl.multiple_of((2 * g + core) * GROUP, GROUP), GROUP)
-            total = acc[t, here, :] + crecv[t, g]
-            crecv[t, g] = total
-            place, low = g // 2, g % 2
-            send1[t, 0, place, low * GROUP : (low + 1) * GROUP, :] = total[:, LEFT].astype(BF16)
-            for high in range(2):
-                send1[t, 1, high * 2 + low, place * HALF : (place + 1) * HALF, :] = total[
-                    high * HALF : (high + 1) * HALF, RIGHT
-                ].astype(BF16)
+    def core_add(t, g):
+        core_copy(t, g).wait_recv()
+        here = pl.ds(pl.multiple_of((2 * g + core) * GROUP, GROUP), GROUP)
+        total = acc[t, here, :] + crecv[t, g]
+        crecv[t, g] = total
+        place, low = g // 2, g % 2
+        send1[t, 0, place, low * GROUP : (low + 1) * GROUP, :] = total[:, LEFT].astype(BF16)
+        for high in range(2):
+            send1[t, 1, high * 2 + low, place * HALF : (place + 1) * HALF, :] = total[
+                high * HALF : (high + 1) * HALF, RIGHT
+            ].astype(BF16)
 
     def start1(t):
         for k in (2, 1, 3):
@@ -344,37 +447,29 @@
         result[pl.ds(1, PIECE, stride=2), :] = total[:, RIGHT]
 
     def out_copy(r):
-        return pltpu.make_async_copy(stage.at[span(r - 1)], out.at[0, r - 1], out_sem.at[r - 1])
-
-    def last(r, count):
-        total = conv(h3, lambda a: wt1[a], r, count, True)
-        here = span(r - 1, count)
-        stage[here, :] = (gv[span(r, count), :].astype(F32) + total * slope[here, :]).astype(BF16)
-        for k in range(count):
-            out_copy(r + k).start()
+        return pltpu.make_async_copy(stage[r], out.at[0, r - 1], out_sem.at[r - 1])
+
+    def last(*rows):
+        def keep(total):
+            for k, r in enumerate(rows):
+                stage[r][...] = (gv[r][...].astype(F32) + total[span(k), :] * slope[r][...]).astype(BF16)
+                out_copy(r).start()
+
+        return conv(h3, lambda a, b: wt1[a, b * CHANS : (b + 1) * CHANS, :], rows, True, keep)
 
     for pair in loads[:4]:
         for copy in pair:
             copy.wait()
-    for copy in weights:
-        copy.wait()
-    turn(wv2, wt2)
-    for r in (1, 2, 3, 4):
-        prep(r)
+    weights[1].wait()
+    weave(turn(wv2, wt2), cots(1, 2, 3, 4))
+    weave(both(backward(2), backward(3)), acted(1, 2, 3, 4))
+    weights[0].wait()
     for pair in loads[4:]:
         for copy in pair:
             copy.wait()
-    convs(2, 2, 0)
-    prep(5)
-    prep(6)
-    convs(4, 2, 1)
-    elem(2, 0, 0)
-    elem(3, 0, 1)
-    prep(7)
-    prep(8)
-    convs(6, 2, 0)
-    elem(4, 1, 0)
-    elem(5, 1, 1)
+    weave(both(forward(2), forward(3)), cots(5, 6, 7, 8) + acted(5, 6))
+    weave(both(forward(4, 5), backward(4, 5)), acted(7, 8) + elem(2))
+    weave(both(forward(6, 7), backward(6, 7)), elem(3, 4, 5), turn(wv1, wt1))
 
     @pl.when(row > 0)
     def _():
@@ -383,8 +478,8 @@
 
     @pl.when(row == 0)
     def _():
-        fv[span(0), :] = jnp.zeros((COLS, CHANS), BF16)
-        gv[span(0), :] = jnp.zeros((COLS, CHANS), BF16)
+        fv[0][...] = jnp.zeros((COLS, CHANS), BF16)
+        gv[0][...] = jnp.zeros((COLS, CHANS), BF16)
 
     @pl.when(row < 7)
     def _():
@@ -393,24 +488,14 @@
 
     @pl.when(row == 7)
     def _():
-        fv[span(ROWS + 1), :] = jnp.zeros((COLS, CHANS), BF16)
-        gv[span(ROWS + 1), :] = jnp.zeros((COLS, CHANS), BF16)
-
-    for a in range(3):
-        grads(1, a, 2, 4, True)
-    prep(0)
-    prep(ROWS + 1)
-    turn(wv1, wt1)
-    convs(1, 1, 1)
-    elem(6, 0, 0)
-    convs(ROWS, 1, 2)
-    elem(7, 0, 1)
-    for a in range(3):
-        grads(1, a, 6, 2, False)
-    elem(1, 1, 0)
-    elem(ROWS, 2, 0)
-    hsend[0] = h3[span(1), CHANS : 2 * CHANS]
-    hsend[1] = h3[span(ROWS), CHANS : 2 * CHANS]
+        fv[ROWS + 1][...] = jnp.zeros((COLS, CHANS), BF16)
+        gv[ROWS + 1][...] = jnp.zeros((COLS, CHANS), BF16)
+
+    weave(one_grads(True, (2, 3), (4, 5)), cots(0, ROWS + 1) + acted(0, ROWS + 1) + elem(6, 7))
+    weave(both(forward(1, ROWS), backward(1, ROWS)), grade(1, 2, 3, 4, 5))
+    weave(one_grads(False, (6, 7)), elem(1, ROWS))
+    hsend[0] = h3[1][:, CHANS : 2 * CHANS]
+    hsend[1] = h3[ROWS][:, CHANS : 2 * CHANS]
 
     @pl.when(row < 7)
     def _():
@@ -420,60 +505,50 @@
     def _():
         h_up.start()
 
-    for a in range(3):
-        grads(1, a, 1, 1, False)
-        grads(1, a, ROWS, 1, False)
-        core_start(1, a)
-        grade(1 + a)
-    grads(0, 0, 1, ROWS, True)
-    core_start(0, 0)
-    grade(4)
-    grade(5)
-    for a in range(3):
-        core_add(1, a)
+    weave(one_grads(False, (1, ROWS)), grade(6, 7, 8))
+    core_start(0)
+    inner = two_grads((2, 3), (4, 5), (6, 7))
+    weave(inner[:9])
+    weave(inner[9:], [functools.partial(core_add, 0, g) for g in range(8)])
+    start1(0)
+    weave(
+        two_edge(1, (1, ROWS), (1, ROWS))
+        + two_edge(2, (2, 1), (1, 0))
+        + two_edge(0, (ROWS - 1, ROWS), (ROWS, ROWS + 1))
+    )
+    core_start(1)
+    start2(0)
+    inner = both(last(2, 3), last(4, 5))
+    weave(inner[:5])
+    weave(inner[5:], [functools.partial(core_add, 1, g) for g in range(8)])
     start1(1)
-    grads(0, 1, 1, ROWS, True)
-    core_start(0, 1)
-    grade(6)
-    grade(7)
-    grads(0, 2, 1, ROWS, True)
-    core_start(0, 2)
-    core_add(0, 0)
-    core_add(0, 1)
-    grade(8)
-    last(2, 2)
-    core_add(0, 2)
-    start1(0)
+    start3(0)
+
+    @pl.when(row > 0)
+    def _():
+        h_down.wait_recv()
+
+    @pl.when(row == 0)
+    def _():
+        hrecv[0] = jnp.zeros((COLS, CHANS), BF16)
+
+    @pl.when(row < 7)
+    def _():
+        h_up.wait_recv()
+
+    @pl.when(row == 7)
+    def _():
+        hrecv[1] = jnp.zeros((COLS, CHANS), BF16)
+
+    inner = both(last(6, 7), last(1, ROWS))
+    weave(single(halo_one, 0, ROWS + 1))
+    weave(inner[:3])
     start2(1)
-    last(4, 2)
+    weave(inner[3:7])
+    finish(0, out_one)
     start3(1)
-    last(6, 2)
-
-    @pl.when(row > 0)
-    def _():
-        h_down.wait_recv()
-
-    @pl.when(row == 0)
-    def _():
-        hrecv[0] = jnp.zeros((COLS, CHANS), BF16)
-
-    @pl.when(row < 7)
-    def _():
-        h_up.wait_recv()
-
-    @pl.when(row == 7)
-    def _():
-        hrecv[1] = jnp.zeros((COLS, CHANS), BF16)
-
-    start2(0)
-    for end in range(2):
-        for lane in (0, 128):
-            widen_grad(end * (ROWS + 1), lane, hrecv[end, :, lane : lane + 128].astype(F32))
-    last(1, 1)
+    weave(inner[7:])
     finish(1, out_two)
-    start3(0)
-    last(ROWS, 1)
-    finish(0, out_one)
 
     @pl.when(row < 7)
     def _():
@@ -503,7 +578,7 @@
     hbm = pl.BlockSpec(memory_space=pl.ANY)
     vmem = pl.BlockSpec(memory_space=pltpu.VMEM)
     dma = pltpu.SemaphoreType.DMA
-    wide_cells = (ROWS + 2) * COLS
+    wide = ROWS + 2
     grad, one, two = pl.pallas_call(
         functools.partial(kernel, scale),
         out_shape=(
@@ -514,23 +589,23 @@
         in_specs=[hbm] * 4,
         out_specs=(hbm, vmem, vmem),
         scratch_shapes=[
-            pltpu.VMEM((wide_cells, CHANS), BF16),
-            pltpu.VMEM((wide_cells, CHANS), BF16),
+            [pltpu.VMEM((COLS, CHANS), BF16)] * wide,
+            [pltpu.VMEM((COLS, CHANS), BF16)] * wide,
             pltpu.VMEM((3, 3, CHANS, CHANS), BF16),
             pltpu.VMEM((3, 3, CHANS, CHANS), BF16),
             pltpu.VMEM((3, WIDE, CHANS), BF16),
             pltpu.VMEM((3, WIDE, CHANS), BF16),
-            pltpu.VMEM((wide_cells, WIDE), BF16),
-            pltpu.VMEM((wide_cells, WIDE), BF16),
-            pltpu.VMEM((wide_cells, WIDE), BF16),
-            pltpu.VMEM((CHANS, wide_cells), BF16),
-            pltpu.VMEM((CHANS, CELLS), BF16),
-            pltpu.VMEM((CELLS, CHANS), F32),
-            pltpu.VMEM((3, 2 * COLS, CHANS), F32),
-            pltpu.VMEM((3, 2 * COLS, CHANS), F32),
+            [pltpu.VMEM((COLS, WIDE), BF16)] * wide,
+            [pltpu.VMEM((COLS, WIDE), BF16)] * wide,
+            [pltpu.VMEM((COLS, WIDE), BF16)] * wide,
+            [pltpu.VMEM((CHANS, COLS), BF16)] * wide,
+            [pltpu.VMEM((CHANS, COLS), BF16)] * wide,
+            [pltpu.VMEM((COLS, CHANS), F32)] * wide,
+            [pltpu.VMEM((COLS, CHANS), F32)] * wide,
+            [pltpu.VMEM((COLS, CHANS), F32)] * wide,
             pltpu.VMEM((2, COLS, CHANS), BF16),
             pltpu.VMEM((2, COLS, CHANS), BF16),
-            pltpu.VMEM((CELLS, CHANS), BF16),
+            [pltpu.VMEM((COLS, CHANS), BF16)] * wide,
             pltpu.VMEM((2, 9 * CHANS, CHANS), F32),
             pltpu.VMEM((2, 8, GROUP, CHANS), F32),
             pltpu.VMEM((2, 2, 4, 2 * GROUP, 128), BF16),

time: 57.8 us -> 57.1 us (0.988)
  Pallas kernels: 53.1 us -> 52.4 us
    pallas_call x1, Pallas kernels: 53.1 us -> 52.4 us  [shards(): pl.pallas_call(functools.partial(kernel, scale), out_shape=(jax.ShapeDtyp...]
where the time goes in v2:
time: 57.1 us; the launch traced here: 57 us
  Pallas kernels  52.4 us (92%)
  local copies, waits for them, and re-layouts  3.89 us (7%)
  between operations  0.66 us (1%)
    pallas_call x1, Pallas kernels, shards(): pl.pallas_call(functools.partial(kernel, scale), out_shape=(jax.ShapeDtyp...  52.4 us
    unnamed x7, local copies, waits for them, and re-layouts  3.89 us

profile of v2, /device:TPU:0, one launch (start us, length us, event | category | flops | bytes accessed | tf_op | source)
XLA Modules:
  0.0 57.0 jit_solution(11498210587090416649)
XLA Ops:
  0.6 52.4 %unit_backward.1 = (bf16[1,8,384,256]{3,2,1,0:T(8,128)(2,1)}, f32[36,128]{1,0:T(8,128)}, f32[36,128]{1,0:T(8,128)}) custom-call(bf16[1,8,384,256]{3,2,1,0:T(8,128)(2,1)} %feat.1, bf16[1,8,384,256]{3,2,1,0:T(8,128)(2,1)} %cot.1, bf16[3,3,256,256]{3,2,1,0:T(8,128)(2,1)} %w_one.1, bf16[3,3,256,256]{3,2,1,0:T(8,128)(2,1)} %w_two.1), custom_call_target="tpu_custom_call" | custom-call | tf_op jit(solution)/shard_map/unit_backward/pallas_call | solution.py:582
  53.1 0.0 copy-start.1
  53.1 0.0 copy-start
  53.1 2.7 %copy.10 = bf16[1,8,384,256]{3,2,1,0:T(8,128)(2,1)} copy(bf16[1,8,384,256]{3,2,1,0:T(8,128)(2,1)} %get-tuple-element.12) | data formatting | bytes 3145728
  55.8 0.0 copy-done.1
  55.8 0.6 %copy.11 = f32[4608]{0:T(1024)} copy(f32[4608]{0:T(1024)S(1)} %bitcast.3) | data formatting | bytes 36864
  56.4 0.0 copy-done
  56.4 0.6 %copy.12 = f32[4608]{0:T(1024)} copy(f32[4608]{0:T(1024)S(1)} %bitcast.2) | data formatting | bytes 36864
Async XLA Ops:
  53.1 2.7 %copy-start.1 = (f32[36,128]{1,0:T(8,128)S(1)}, f32[36,128]{1,0:T(8,128)}, u32[]{:S(2)}) copy-start(f32[36,128]{1,0:T(8,128)} %get-tuple-element.7) | copy-start | bytes 55300
  53.1 3.3 %copy-start = (f32[36,128]{1,0:T(8,128)S(1)}, f32[36,128]{1,0:T(8,128)}, u32[]{:S(2)}) copy-start(f32[36,128]{1,0:T(8,128)} %get-tuple-element.8) | copy-start | bytes 55300

commit v3 on v2

--- a/solution.py
+++ b/solution.py
@@ -151,7 +151,6 @@
             peers.append(peer(k)[1])
     for peer in peers:
         pl.semaphore_signal(barrier, inc=1, device_id=peer, device_id_type=MESH)
-    pl.semaphore_wait(barrier, len(peers))
 
     def halo(which, down, src, dst):
         return pltpu.make_async_remote_copy(
@@ -173,16 +172,6 @@
     ]
     h_down = halo(2, 1, hsend.at[1], hrecv.at[0])
     h_up = halo(2, 0, hsend.at[0], hrecv.at[1])
-
-    @pl.when(row < 7)
-    def _():
-        for copy in halos_down:
-            copy.start()
-
-    @pl.when(row > 0)
-    def _():
-        for copy in halos_up:
-            copy.start()
 
     def turn(source, target):
         def block(a, b):
@@ -333,9 +322,9 @@
         terms = [[(at, (p + a - 1, q + a - 1)) for a in range(3)] + [(h3, (p, q))] for p, q in pairs]
         return grads(0, fresh, terms)
 
-    def two_grads(*pairs):
+    def two_grads(fresh, *pairs):
         terms = [[(gt, (p + a - 1, q + a - 1)) for a in range(3)] + [(g3, (p, q))] for p, q in pairs]
-        return grads(1, True, terms)
+        return grads(1, fresh, terms)
 
     def two_edge(a, left, right):
         return grads(1, False, [[(gt, left), (g3, right)]], (a,))
@@ -376,8 +365,8 @@
     HALF = GROUP // 2
     LEFT, RIGHT = slice(0, 128), slice(128, 256)
 
-    def core_start(t):
-        for g in range(8):
+    def core_start(t, groups):
+        for g in groups:
             core_copy(t, g).start()
 
     def core_add(t, g):
@@ -462,6 +451,18 @@
             copy.wait()
     weights[1].wait()
     weave(turn(wv2, wt2), cots(1, 2, 3, 4))
+    pl.semaphore_wait(barrier, len(peers))
+
+    @pl.when(row < 7)
+    def _():
+        for copy in halos_down:
+            copy.start()
+
+    @pl.when(row > 0)
+    def _():
+        for copy in halos_up:
+            copy.start()
+
     weave(both(backward(2), backward(3)), acted(1, 2, 3, 4))
     weights[0].wait()
     for pair in loads[4:]:
@@ -470,6 +471,7 @@
     weave(both(forward(2), forward(3)), cots(5, 6, 7, 8) + acted(5, 6))
     weave(both(forward(4, 5), backward(4, 5)), acted(7, 8) + elem(2))
     weave(both(forward(6, 7), backward(6, 7)), elem(3, 4, 5), turn(wv1, wt1))
+    weave(one_grads(True, (2, 3), (4, 5)), elem(6, 7))
 
     @pl.when(row > 0)
     def _():
@@ -491,9 +493,9 @@
         fv[ROWS + 1][...] = jnp.zeros((COLS, CHANS), BF16)
         gv[ROWS + 1][...] = jnp.zeros((COLS, CHANS), BF16)
 
-    weave(one_grads(True, (2, 3), (4, 5)), cots(0, ROWS + 1) + acted(0, ROWS + 1) + elem(6, 7))
+    weave(one_grads(False, (6, 7)), cots(0, ROWS + 1) + acted(0, ROWS + 1))
     weave(both(forward(1, ROWS), backward(1, ROWS)), grade(1, 2, 3, 4, 5))
-    weave(one_grads(False, (6, 7)), elem(1, ROWS))
+    weave(two_grads(True, (4, 5)), elem(1, ROWS))
     hsend[0] = h3[1][:, CHANS : 2 * CHANS]
     hsend[1] = h3[ROWS][:, CHANS : 2 * CHANS]
 
@@ -506,48 +508,47 @@
         h_up.start()
 
     weave(one_grads(False, (1, ROWS)), grade(6, 7, 8))
-    core_start(0)
-    inner = two_grads((2, 3), (4, 5), (6, 7))
-    weave(inner[:9])
-    weave(inner[9:], [functools.partial(core_add, 0, g) for g in range(8)])
+    core_start(0, range(8))
+    inner = two_grads(False, (2, 3), (6, 7))
+    weave(inner[:4])
+    weave(inner[4:], [functools.partial(core_add, 0, g) for g in range(8)])
     start1(0)
-    weave(
-        two_edge(1, (1, ROWS), (1, ROWS))
-        + two_edge(2, (2, 1), (1, 0))
-        + two_edge(0, (ROWS - 1, ROWS), (ROWS, ROWS + 1))
-    )
-    core_start(1)
+    weave(two_edge(0, (ROWS - 1, ROWS), (ROWS, ROWS + 1)))
+    core_start(1, (0, 1))
+    weave(two_edge(1, (1, ROWS), (1, ROWS)))
+    core_start(1, (2, 3, 4))
+    weave(two_edge(2, (2, 1), (1, 0)))
+    core_start(1, (5, 6, 7))
+    inner = both(last(2, 3), last(4, 5))
+    weave(inner[:5], [functools.partial(core_add, 1, g) for g in range(5)])
+    for g in (5, 6, 7):
+        core_add(1, g)
+    start1(1)
+    weave(inner[5:])
+
+    @pl.when(row > 0)
+    def _():
+        h_down.wait_recv()
+
+    @pl.when(row == 0)
+    def _():
+        hrecv[0] = jnp.zeros((COLS, CHANS), BF16)
+
+    @pl.when(row < 7)
+    def _():
+        h_up.wait_recv()
+
+    @pl.when(row == 7)
+    def _():
+        hrecv[1] = jnp.zeros((COLS, CHANS), BF16)
+
+    weave(single(halo_one, 0, ROWS + 1))
+    weave(both(last(6, 7), last(1, ROWS)))
     start2(0)
-    inner = both(last(2, 3), last(4, 5))
-    weave(inner[:5])
-    weave(inner[5:], [functools.partial(core_add, 1, g) for g in range(8)])
-    start1(1)
+    start2(1)
     start3(0)
-
-    @pl.when(row > 0)
-    def _():
-        h_down.wait_recv()
-
-    @pl.when(row == 0)
-    def _():
-        hrecv[0] = jnp.zeros((COLS, CHANS), BF16)
-
-    @pl.when(row < 7)
-    def _():
-        h_up.wait_recv()
-
-    @pl.when(row == 7)
-    def _():
-        hrecv[1] = jnp.zeros((COLS, CHANS), BF16)
-
-    inner = both(last(6, 7), last(1, ROWS))
-    weave(single(halo_one, 0, ROWS + 1))
-    weave(inner[:3])
-    start2(1)
-    weave(inner[3:7])
+    start3(1)
     finish(0, out_one)
-    start3(1)
-    weave(inner[7:])
     finish(1, out_two)
 
     @pl.when(row < 7)

time: 57.1 us -> 51.8 us (0.907)
  Pallas kernels: 52.4 us -> 47.1 us
    pallas_call x1, Pallas kernels: 52.4 us -> 47.1 us  [shards(): pl.pallas_call(functools.partial(kernel, scale), out_shape=(jax.ShapeDtyp...]
where the time goes in v3:
time: 51.8 us; the launch traced here: 51.6 us
  Pallas kernels  47.1 us (91%)
  local copies, waits for them, and re-layouts  3.89 us (8%)
  between operations  0.66 us (1%)
    pallas_call x1, Pallas kernels, shards(): pl.pallas_call(functools.partial(kernel, scale), out_shape=(jax.ShapeDtyp...  47.1 us
    unnamed x7, local copies, waits for them, and re-layouts  3.89 us

profile of v3, /device:TPU:0, one launch (start us, length us, event | category | flops | bytes accessed | tf_op | source)
XLA Modules:
  0.0 51.6 jit_solution(1854481576080715399)
XLA Ops:
  0.6 47.1 %unit_backward.1 = (bf16[1,8,384,256]{3,2,1,0:T(8,128)(2,1)}, f32[36,128]{1,0:T(8,128)}, f32[36,128]{1,0:T(8,128)}) custom-call(bf16[1,8,384,256]{3,2,1,0:T(8,128)(2,1)} %feat.1, bf16[1,8,384,256]{3,2,1,0:T(8,128)(2,1)} %cot.1, bf16[3,3,256,256]{3,2,1,0:T(8,128)(2,1)} %w_one.1, bf16[3,3,256,256]{3,2,1,0:T(8,128)(2,1)} %w_two.1), custom_call_target="tpu_custom_call" | custom-call | tf_op jit(solution)/shard_map/unit_backward/pallas_call | solution.py:583
  47.7 0.0 copy-start.1
  47.7 0.0 copy-start
  47.7 2.7 %copy.10 = bf16[1,8,384,256]{3,2,1,0:T(8,128)(2,1)} copy(bf16[1,8,384,256]{3,2,1,0:T(8,128)(2,1)} %get-tuple-element.12) | data formatting | bytes 3145728
  50.4 0.0 copy-done.1
  50.4 0.6 %copy.11 = f32[4608]{0:T(1024)} copy(f32[4608]{0:T(1024)S(1)} %bitcast.3) | data formatting | bytes 36864
  51.0 0.0 copy-done
  51.0 0.6 %copy.12 = f32[4608]{0:T(1024)} copy(f32[4608]{0:T(1024)S(1)} %bitcast.2) | data formatting | bytes 36864
Async XLA Ops:
  47.7 2.7 %copy-start.1 = (f32[36,128]{1,0:T(8,128)S(1)}, f32[36,128]{1,0:T(8,128)}, u32[]{:S(2)}) copy-start(f32[36,128]{1,0:T(8,128)} %get-tuple-element.7) | copy-start | bytes 55300
  47.7 3.3 %copy-start = (f32[36,128]{1,0:T(8,128)S(1)}, f32[36,128]{1,0:T(8,128)}, u32[]{:S(2)}) copy-start(f32[36,128]{1,0:T(8,128)} %get-tuple-element.8) | copy-start | bytes 55300
